TPU v7x, 128 devices: a whole 4x4x4 slice. The times are simulated.
128 devices in a mesh: leaf: 32 (over x, y, core), chain: 4 (over z).
Axes of the slice: x: 4, y: 4, z: 4, core: 2. Of those that a mesh axis runs over, the one named last changes fastest.
Arguments:
- right_side: float32 [32, 4096, 1024], P('leaf', 'chain'), may hold values from -6 to 6
- lower_rows: bfloat16 [32, 4096, 4096], P('leaf', 'chain'), may hold values from -0.09375 to 0.09375
- block_inverse: bfloat16 [32, 4096, 1024], P('leaf', 'chain'), may hold values from -0.1875 to 0.1875
- ancestor_cols: bfloat16 [32, 3072, 4096], P('leaf', None, 'chain'), may hold values from -0.09375 to 0.09375
- pattern: int32 [32, 24], P('leaf'), may hold values 0 or 1
- ancestor_side: float32 [3072, 1024], P('chain'), may hold values from -24 to 24
- ancestor_inverse: bfloat16 [3072, 768], P('chain'), may hold values from -0.21875 to 0.21875
Outputs:
- solution: float32 [32, 4096, 1024], P('leaf', 'chain')
- ancestor_solution: float32 [4, 768, 1024], P('chain', 'leaf')
All inputs are finite; a program needn't handle non-finite values. No bound on the sum of `pattern` on one device may be relied on, other than what follows from the above.
Results may differ from a plain program's by a relative error of at most 0.0065.
Values may be sent and summed in bfloat16 or wider, within the bound.
A program may use at most 128 MiB of HBM per device.

v0:
```python
import jax
import jax.numpy as jnp
from jax import lax
from jax.sharding import PartitionSpec as P

ROWBLK = 128


def broadcast(value, axis, root):
    mine = lax.axis_index(axis) == root
    return lax.psum(jnp.where(mine, value, jnp.zeros_like(value)), axis)


def from_partner(value, axis, stride):
    mask = 2**stride
    pairs = [(source, source ^ mask) for source in range(lax.axis_size(axis))]
    return lax.ppermute(value, axis, pairs)


def local(
    right_side, lower_rows, block_inverse, ancestor_cols, pattern, ancestor_side, ancestor_inverse
):
    rhs_rows = right_side[0]
    lower = lower_rows[0]
    inverse = block_inverse[0]
    flags = pattern[0]
    block_rows = lower.shape[0]
    chain_count = lax.axis_size("chain")
    position = lax.axis_index("chain")
    owned_rows = ancestor_side.shape[0]
    row_flags = jnp.repeat(flags.astype(jnp.float32), ROWBLK)
    pending = jnp.zeros(rhs_rows.shape, jnp.float32)
    solved = jnp.zeros(rhs_rows.shape, jnp.float32)
    arrivals = []
    for chain_step in range(chain_count):
        current = pending
        candidate = lax.cond(
            position == chain_step,
            lambda: jnp.dot(
                inverse,
                (rhs_rows - current).astype(jnp.bfloat16),
                preferred_element_type=jnp.float32,
            ),
            lambda: jnp.zeros(rhs_rows.shape, jnp.float32),
        )
        solved = solved + candidate
        arrived = broadcast(candidate.astype(jnp.bfloat16), "chain", chain_step)
        arrivals.append(arrived)
        if chain_step + 1 < chain_count:
            column_block = lower[:, chain_step * block_rows : (chain_step + 1) * block_rows]
            pending = lax.cond(
                position > chain_step,
                lambda: current
                + jnp.dot(column_block, arrived, preferred_element_type=jnp.float32),
                lambda: current,
            )
    solved_low = solved.astype(jnp.bfloat16)
    columns = ancestor_cols[0]
    product = jnp.dot(columns, solved_low, preferred_element_type=jnp.float32)
    partial_value = lax.psum_scatter(
        product * row_flags[:, None], "chain", scatter_dimension=0, tiled=True
    )
    levels = lax.axis_size("leaf").bit_length() - 1
    for level in range(levels):
        partial_value = partial_value + from_partner(partial_value, "leaf", level)
    share_rows = owned_rows // lax.axis_size("leaf")
    leaf_position = lax.axis_index("leaf")
    inverse_share = lax.dynamic_slice_in_dim(
        ancestor_inverse, leaf_position * share_rows, share_rows, 0
    )
    ancestor_solution = jnp.dot(
        inverse_share,
        (ancestor_side - partial_value).astype(jnp.bfloat16),
        preferred_element_type=jnp.float32,
    )
    return (solved[None], ancestor_solution[None])


def solution(mesh):
    return jax.shard_map(
        local,
        mesh=mesh,
        in_specs=(
            P("leaf", "chain", None),
            P("leaf", "chain", None),
            P("leaf", "chain", None),
            P("leaf", None, "chain"),
            P("leaf", None),
            P("chain", None),
            P("chain", None),
        ),
        out_specs=(P("leaf", "chain", None), P("chain", "leaf", None)),
        check_vma=False,
    )
```

profile of v0, /device:TPU:0, one launch (start us, length us, event | category | flops | bytes accessed | tf_op | source)
XLA Modules:
  0.0 701.0 jit_solution(8203343773028368888)
XLA Ops:
  7.2 7.3 %conditional.7 = (f32[1024,1024]{1,0:T(8,128)}, bf16[1024,1024]{1,0:T(8,128)(2,1)S(1)}) conditional(s32[]{:T(128)} %convert_element_type.63, () %tuple.62, (f32[1024,1024]{1,0:T(8,128)}, bf16[1024,1024]{1,0:T(8,128)(2,1)}) %tuple.117), branch_computations={%region_0.0_spmd, %region_1.0_spmd} | conditional | flops 2149580800 | bytes 12582928 | solution.py:37
  7.3 7.2 %fusion.20 = (bf16[1024,1024]{1,0:T(8,128)(2,1)S(1)}, f32[1024,1024]{1,0:T(8,128)}) fusion(bf16[1024,1024]{1,0:T(8,128)(2,1)} %get-tuple-element.59, f32[1024,1024]{1,0:T(8,128)} %get-tuple-element.60), kind=kOutput, calls=%fused_computation.30 | convolution fusion | flops 2149580800 | bytes 12582912 | tf_op jit(solution)/shard_map/cond/branch_1_fun/dot_general | solution.py:39
  16.0 58.1 %all-reduce.4.cloned.1.call-done = bf16[1024,1024]{1,0:T(8,128)(2,1)} async-done(((bf16[1024,1024]{1,0:T(8,128)(2,1)}), bf16[1024,1024]{1,0:T(8,128)(2,1)}) %all-reduce.4.cloned.1.call-update) | async-done | bytes 2097168 | tf_op jit(solution)/shard_map/psum | solution.py:11
  74.1 2.6 conditional.8
  74.1 2.5 broadcast.24
  76.6 2.8 conditional.9
  76.6 2.5 broadcast.25.clone
  79.4 1.4 broadcast_select_fusion.1
  80.9 76.0 %all-reduce.6.cloned.1.call-done = bf16[1024,1024]{1,0:T(8,128)(2,1)} async-done(((bf16[1024,1024]{1,0:T(8,128)(2,1)}), bf16[1024,1024]{1,0:T(8,128)(2,1)}) %all-reduce.6.cloned.1.call-update) | async-done | bytes 2097168 | tf_op jit(solution)/shard_map/psum | solution.py:11
  156.9 2.9 conditional.11
  156.9 2.5 broadcast.27.clone
  161.4 80.8 %all-reduce.8.cloned.1.call-done = bf16[1024,1024]{1,0:T(8,128)(2,1)} async-done(((bf16[1024,1024]{1,0:T(8,128)(2,1)}), bf16[1024,1024]{1,0:T(8,128)(2,1)}) %all-reduce.8.cloned.1.call-update) | async-done | bytes 2097168 | tf_op jit(solution)/shard_map/psum | solution.py:11
  242.3 1.6 copy-done.2
  243.8 2.5 conditional.13
  243.8 2.5 broadcast.29.clone
  246.3 7.9 %add_add_fusion = f32[1024,1024]{1,0:T(8,128)S(1)} fusion(f32[1024,1024]{1,0:T(8,128)} %get-tuple-element.98, f32[1024,1024]{1,0:T(8,128)} %get-tuple-element.96, f32[1024,1024]{1,0:T(8,128)} %get-tuple-element.86, f32[1024,1024]{1,0:T(8,128)} %get-tuple-element.94), kind=kLoop, calls=%fused_computation.18 | loop fusion | flops 3145728 | bytes 20971520 | tf_op jit(solution)/shard_map/add | solution.py:46
  254.2 2.0 copy-done.1
  256.2 12.4 %multiply_bitcast_fusion = f32[3072,1024]{0,1:T(8,128)} fusion(bf16[1,3072,1024]{2,1,0:T(8,128)(2,1)} %param.24, f32[3072]{0:T(1024)S(1)} %broadcast_bitcast_fusion, f32[1024,1024]{1,0:T(8,128)S(1)} %add_add_fusion), kind=kOutput, calls=%fused_computation.16 | convolution fusion | flops 6446645248 | bytes 23080960 | tf_op jit(solution)/shard_map/dot_general | solution.py:59
  268.6 130.9 %reduce-scatter.2.cloned.1.call-done = f32[768,1024]{0,1:T(8,128)} async-done(((f32[3072,1024]{0,1:T(8,128)}), f32[768,1024]{0,1:T(8,128)}) %reduce-scatter.2.cloned.1.call-update) | async-done | bytes 3145744 | tf_op jit(solution)/shard_map/reduce_scatter | solution.py:60
  399.5 5.9 collective-permute-done
  405.4 2.3 add.45
  407.6 1.6 collective-permute-start.1
  409.2 68.7 %collective-permute-done.1 = f32[768,1024]{0,1:T(8,128)S(1)} collective-permute-done((f32[768,1024]{0,1:T(8,128)S(1)}, f32[768,1024]{0,1:T(8,128)S(1)}, u32[]{:S(2)}, u32[]{:S(2)}) %collective-permute-start.1) | collective-permute-done | bytes 3145760 | tf_op jit(solution)/shard_map/ppermute | solution.py:17
  478.2 3.1 collective-permute-start.2
  481.3 67.8 %collective-permute-done.2 = f32[768,1024]{0,1:T(8,128)S(1)} collective-permute-done((f32[768,1024]{0,1:T(8,128)S(1)}, f32[768,1024]{0,1:T(8,128)S(1)}, u32[]{:S(2)}, u32[]{:S(2)}) %collective-permute-start.2) | collective-permute-done | bytes 3145760 | tf_op jit(solution)/shard_map/ppermute | solution.py:17
  549.5 1.5 collective-permute-start.3
  551.1 67.0 %collective-permute-done.3 = f32[768,1024]{0,1:T(8,128)S(1)} collective-permute-done((f32[768,1024]{0,1:T(8,128)S(1)}, f32[768,1024]{0,1:T(8,128)S(1)}, u32[]{:S(2)}, u32[]{:S(2)}) %collective-permute-start.3) | collective-permute-done | bytes 3145760 | tf_op jit(solution)/shard_map/ppermute | solution.py:17
  618.0 2.1 add.48
  620.1 3.0 collective-permute-start.4
  623.1 3.5 copy.14
  626.6 62.9 %collective-permute-done.4 = f32[768,1024]{0,1:T(8,128)} collective-permute-done((f32[768,1024]{0,1:T(8,128)}, f32[768,1024]{0,1:T(8,128)}, u32[]{:S(2)}, u32[]{:S(2)}) %collective-permute-start.4) | collective-permute-done | bytes 3145760 | tf_op jit(solution)/shard_map/ppermute | solution.py:17
  689.5 4.9 fusion.17
  (25 shorter events, 4.5 us)
Async XLA Ops:
  7.2 682.3 %copy-start = (bf16[768,768]{1,0:T(8,128)(2,1)S(1)}, bf16[768,768]{1,0:T(8,128)(2,1)}, u32[]{:S(2)}) copy-start(bf16[768,768]{1,0:T(8,128)(2,1)} %param.27) | copy-start | bytes 3538948
  7.2 66.9 %all-reduce.4.cloned.1.call-start = ((), (), s32[]{:S(2)}) async-start(), calls=%async_computation.1 | async-start | bytes 4194304 | tf_op jit(solution)/shard_map/psum | solution.py:11
  16.0 140.9 %all-reduce.6.cloned.1.call-start = ((), (), s32[]{:S(2)}) async-start(), calls=%async_computation.2 | async-start | bytes 4194304 | tf_op jit(solution)/shard_map/psum | solution.py:11
  80.9 161.4 %all-reduce.8.cloned.1.call-start = ((), (), s32[]{:S(2)}) async-start(), calls=%async_computation.3 | async-start | bytes 4194304 | tf_op jit(solution)/shard_map/psum | solution.py:11
  159.8 1.5 copy-start.3
  161.3 238.2 %reduce-scatter.2.cloned.1.call-start = ((), (), s32[]{:S(2)}) async-start(), calls=%async_computation.4 | async-start | bytes 15728640 | tf_op jit(solution)/shard_map/reduce_scatter | solution.py:60
  242.3 1.6 copy-start.2
  254.2 2.0 copy-start.1
  399.5 5.9 collective-permute-start
  407.6 70.2 %collective-permute-start.1 = (f32[768,1024]{0,1:T(8,128)S(1)}, f32[768,1024]{0,1:T(8,128)S(1)}, u32[]{:S(2)}, u32[]{:S(2)}) collective-permute-start(f32[768,1024]{0,1:T(8,128)S(1)} %add.45), channel_id=1, source_target_pairs={{0,8},{4,12},{8,0},{12,4},{16,24},{20,28},{24,16},{28,20},{32,40},... | collective-permute-start | bytes 9437192 | tf_op jit(solution)/shard_map/ppermute | solution.py:17
  478.2 70.9 %collective-permute-start.2 = (f32[768,1024]{0,1:T(8,128)S(1)}, f32[768,1024]{0,1:T(8,128)S(1)}, u32[]{:S(2)}, u32[]{:S(2)}) collective-permute-start(f32[768,1024]{0,1:T(8,128)S(1)} %add.46), channel_id=1, source_target_pairs={{0,16},{4,20},{8,24},{12,28},{16,0},{20,4},{24,8},{28,12},{32,48},... | collective-permute-start | bytes 9437192 | tf_op jit(solution)/shard_map/ppermute | solution.py:17
  549.5 68.5 %collective-permute-start.3 = (f32[768,1024]{0,1:T(8,128)S(1)}, f32[768,1024]{0,1:T(8,128)S(1)}, u32[]{:S(2)}, u32[]{:S(2)}) collective-permute-start(f32[768,1024]{0,1:T(8,128)S(1)} %add.47), channel_id=1, source_target_pairs={{0,32},{4,36},{8,40},{12,44},{16,48},{20,52},{24,56},{28,60},{32,0... | collective-permute-start | bytes 9437192 | tf_op jit(solution)/shard_map/ppermute | solution.py:17
  620.1 69.4 %collective-permute-start.4 = (f32[768,1024]{0,1:T(8,128)}, f32[768,1024]{0,1:T(8,128)}, u32[]{:S(2)}, u32[]{:S(2)}) collective-permute-start(f32[768,1024]{0,1:T(8,128)} %add.48), channel_id=1, source_target_pairs={{0,64},{4,68},{8,72},{12,76},{16,80},{20,84},{24,88},{28,92},{32,9... | collective-permute-start | bytes 9437192 | tf_op jit(solution)/shard_map/ppermute | solution.py:17
Sparse Core Ops, SparseCore 0:
  16.1 57.9 all-reduce.3
  81.0 75.8 all-reduce.5
  161.4 80.8 all-reduce.7
  268.7 130.7 reduce-scatter.1
where the time goes:
time: 701 us
  waiting for transfers between devices  618 us (88%)
  matrix products  24.6 us (4%)
  local copies, waits for them, and re-layouts  17.7 us (3%)
  other arithmetic  17.3 us (2%)
  between operations  13.9 us (2%)
  starting transfers between devices  9.34 us (1%)
    ppermute x5, waiting for transfers between devices, from_partner(): return lax.ppermute(value, axis, pairs)  272 us
    psum x3, waiting for transfers between devices, broadcast(): return lax.psum(jnp.where(mine, value, jnp.zeros_like(value)), axis)  215 us
    reduce_scatter x1, waiting for transfers between devices, local(): lax.psum_scatter(product * row_flags[:, None], 'chain', scatter_dimension...  131 us
  transfers between devices with their start and end apart: 9, of which 9 were waited for; matrix products, arithmetic and copies ran while one was open for 1% of the time, Pallas kernels for 0%

commit v1 on v0

--- a/solution.py
+++ b/solution.py
@@ -2,13 +2,19 @@
 import jax.numpy as jnp
 from jax import lax
 from jax.sharding import PartitionSpec as P
+from jax.lax import all_gather
 
 ROWBLK = 128
 
 
+def produce_marks(page, ax_name):
+    parts_out = all_gather(page, axis_name=ax_name)
+    return jnp.sum(parts_out, 0)
+
+
 def broadcast(value, axis, root):
     mine = lax.axis_index(axis) == root
-    return lax.psum(jnp.where(mine, value, jnp.zeros_like(value)), axis)
+    return produce_marks(jnp.where(mine, value, jnp.zeros_like(value)), axis)
 
 
 def from_partner(value, axis, stride):

time: 701 us -> 853 us (1.22)
  waiting for transfers between devices: 618 us -> 766 us
    all_gather x0 -> x3, waiting for transfers between devices: none -> 334 us  [produce_marks(): parts_out = all_gather(page, axis_name=ax_name)]
    psum x3 -> x0, waiting for transfers between devices: 215 us -> none  [broadcast(): return lax.psum(jnp.where(mine, value, jnp.zeros_like(value)), axis)]
    reduce_scatter x1, waiting for transfers between devices: 131 us -> 159 us  [local(): lax.psum_scatter(product * row_flags[:, None], 'chain', scatter_dimension...]
  transfers between devices with their start and end apart: 9 -> 9, of which waited for: 9 -> 9; matrix products, arithmetic and copies ran while one was open for 1% -> 0% of each run, Pallas kernels for 0% -> 0%
where the time goes in v1:
time: 853 us; the launch traced here: 851 us
  waiting for transfers between devices  766 us (90%)
  matrix products  25.3 us (3%)
  local copies, waits for them, and re-layouts  19 us (2%)
  other arithmetic  17.6 us (2%)
  between operations  13.9 us (2%)
  starting transfers between devices  9.34 us (1%)
    all_gather x3, waiting for transfers between devices, produce_marks(): parts_out = all_gather(page, axis_name=ax_name)  334 us
    ppermute x5, waiting for transfers between devices, from_partner(): return lax.ppermute(value, axis, pairs)  272 us
    reduce_scatter x1, waiting for transfers between devices, local(): lax.psum_scatter(product * row_flags[:, None], 'chain', scatter_dimension...  159 us
  transfers between devices with their start and end apart: 9, of which 9 were waited for; matrix products, arithmetic and copies ran while one was open for 0% of the time, Pallas kernels for 0%

profile of v1, /device:TPU:0, one launch (start us, length us, event | category | flops | bytes accessed | tf_op | source)
XLA Modules:
  0.0 850.8 jit_solution(11306244337109551330)
XLA Ops:
  7.2 10.8 %conditional.7 = (f32[1024,1024]{1,0:T(8,128)}, bf16[1024,1024]{0,1:T(8,128)(2,1)S(1)}) conditional(s32[]{:T(128)} %convert_element_type.69, () %tuple.62, (f32[1024,1024]{1,0:T(8,128)}, bf16[1024,1024]{1,0:T(8,128)(2,1)}) %tuple.118), branch_computations={%region_0.0_spmd, %region_1.0_spmd} | conditional | flops 2149580800 | bytes 16777232 | solution.py:43
  7.3 7.9 fusion.20
  15.2 2.9 copy.26
  18.1 1.5 broadcast_select_fusion.2
  19.7 82.4 %all-gather.7.cloned.1.call-done = bf16[4096,1024]{0,1:T(8,128)(2,1)} async-done(((bf16[1024,1024]{0,1:T(8,128)(2,1)}), bf16[4096,1024]{0,1:T(8,128)(2,1)}) %all-gather.7.cloned.1.call-update) | async-done | bytes 8388624 | tf_op jit(solution)/shard_map/all_gather | solution.py:11
  102.1 2.5 conditional.8
  102.1 2.5 broadcast.24
  104.6 2.8 conditional.9
  104.6 2.5 broadcast.25.clone
  109.0 123.5 %all-gather.9.cloned.1.call-done = bf16[4096,1024]{0,1:T(8,128)(2,1)} async-done(((bf16[1024,1024]{0,1:T(8,128)(2,1)}), bf16[4096,1024]{0,1:T(8,128)(2,1)}) %all-gather.9.cloned.1.call-update) | async-done | bytes 8388624 | tf_op jit(solution)/shard_map/all_gather | solution.py:11
  232.5 2.8 conditional.11
  232.5 2.5 broadcast.27.clone
  237.0 128.4 %all-gather.11.cloned.1.call-done = bf16[4096,1024]{0,1:T(8,128)(2,1)} async-done(((bf16[1024,1024]{0,1:T(8,128)(2,1)}), bf16[4096,1024]{0,1:T(8,128)(2,1)}) %all-gather.11.cloned.1.call-update) | async-done | bytes 8388624 | tf_op jit(solution)/shard_map/all_gather | solution.py:11
  365.4 2.5 conditional.13
  365.4 2.5 broadcast.29.clone
  367.9 7.9 add_add_fusion
  375.8 2.0 copy-done.1
  377.8 12.4 %multiply_bitcast_fusion = f32[3072,1024]{0,1:T(8,128)} fusion(bf16[1,3072,1024]{2,1,0:T(8,128)(2,1)} %param.24, f32[3072]{0:T(1024)S(1)} %broadcast_bitcast_fusion, f32[1024,1024]{1,0:T(8,128)S(1)} %add_add_fusion), kind=kOutput, calls=%fused_computation.16 | convolution fusion | flops 6446645248 | bytes 23080960 | tf_op jit(solution)/shard_map/dot_general | solution.py:65
  390.2 159.1 %reduce-scatter.2.cloned.1.call-done = f32[768,1024]{0,1:T(8,128)} async-done(((f32[3072,1024]{0,1:T(8,128)}), f32[768,1024]{0,1:T(8,128)}) %reduce-scatter.2.cloned.1.call-update) | async-done | bytes 3145744 | tf_op jit(solution)/shard_map/reduce_scatter | solution.py:66
  549.3 5.9 collective-permute-done
  555.2 2.3 add.39
  557.5 1.6 collective-permute-start.1
  559.0 68.7 %collective-permute-done.1 = f32[768,1024]{0,1:T(8,128)S(1)} collective-permute-done((f32[768,1024]{0,1:T(8,128)S(1)}, f32[768,1024]{0,1:T(8,128)S(1)}, u32[]{:S(2)}, u32[]{:S(2)}) %collective-permute-start.1) | collective-permute-done | bytes 3145760 | tf_op jit(solution)/shard_map/ppermute | solution.py:23
  628.1 3.1 collective-permute-start.2
  631.2 67.8 %collective-permute-done.2 = f32[768,1024]{0,1:T(8,128)S(1)} collective-permute-done((f32[768,1024]{0,1:T(8,128)S(1)}, f32[768,1024]{0,1:T(8,128)S(1)}, u32[]{:S(2)}, u32[]{:S(2)}) %collective-permute-start.2) | collective-permute-done | bytes 3145760 | tf_op jit(solution)/shard_map/ppermute | solution.py:23
  699.3 1.5 collective-permute-start.3
  700.9 67.0 %collective-permute-done.3 = f32[768,1024]{0,1:T(8,128)S(1)} collective-permute-done((f32[768,1024]{0,1:T(8,128)S(1)}, f32[768,1024]{0,1:T(8,128)S(1)}, u32[]{:S(2)}, u32[]{:S(2)}) %collective-permute-start.3) | collective-permute-done | bytes 3145760 | tf_op jit(solution)/shard_map/ppermute | solution.py:23
  767.9 2.1 add.42
  769.9 3.0 collective-permute-start.4
  772.9 3.5 copy.21
  776.4 62.9 %collective-permute-done.4 = f32[768,1024]{0,1:T(8,128)} collective-permute-done((f32[768,1024]{0,1:T(8,128)}, f32[768,1024]{0,1:T(8,128)}, u32[]{:S(2)}, u32[]{:S(2)}) %collective-permute-start.4) | collective-permute-done | bytes 3145760 | tf_op jit(solution)/shard_map/ppermute | solution.py:23
  839.3 4.9 fusion.17
  (24 shorter events, 4.7 us)
Async XLA Ops:
  7.2 832.1 %copy-start = (bf16[768,768]{1,0:T(8,128)(2,1)S(1)}, bf16[768,768]{1,0:T(8,128)(2,1)}, u32[]{:S(2)}) copy-start(bf16[768,768]{1,0:T(8,128)(2,1)} %param.27) | copy-start | bytes 3538948
  7.2 94.9 %all-gather.7.cloned.1.call-start = ((), (), s32[]{:S(2)}) async-start(), calls=%async_computation.2 | async-start | bytes 10485760 | tf_op jit(solution)/shard_map/all_gather | solution.py:11
  19.6 212.9 %all-gather.9.cloned.1.call-start = ((), (), s32[]{:S(2)}) async-start(), calls=%async_computation.3 | async-start | bytes 10485760 | tf_op jit(solution)/shard_map/all_gather | solution.py:11
  108.9 256.4 %all-gather.11.cloned.1.call-start = ((), (), s32[]{:S(2)}) async-start(), calls=%async_computation.4 | async-start | bytes 10485760 | tf_op jit(solution)/shard_map/all_gather | solution.py:11
  235.3 1.6 copy-start.2
  236.9 312.5 %reduce-scatter.2.cloned.1.call-start = ((), (), s32[]{:S(2)}) async-start(), calls=%async_computation.1 | async-start | bytes 15728640 | tf_op jit(solution)/shard_map/reduce_scatter | solution.py:66
  375.8 2.0 copy-start.1
  549.3 5.9 collective-permute-start
  557.5 70.2 %collective-permute-start.1 = (f32[768,1024]{0,1:T(8,128)S(1)}, f32[768,1024]{0,1:T(8,128)S(1)}, u32[]{:S(2)}, u32[]{:S(2)}) collective-permute-start(f32[768,1024]{0,1:T(8,128)S(1)} %add.39), channel_id=1, source_target_pairs={{0,8},{4,12},{8,0},{12,4},{16,24},{20,28},{24,16},{28,20},{32,40},... | collective-permute-start | bytes 9437192 | tf_op jit(solution)/shard_map/ppermute | solution.py:23
  628.1 70.9 %collective-permute-start.2 = (f32[768,1024]{0,1:T(8,128)S(1)}, f32[768,1024]{0,1:T(8,128)S(1)}, u32[]{:S(2)}, u32[]{:S(2)}) collective-permute-start(f32[768,1024]{0,1:T(8,128)S(1)} %add.40), channel_id=1, source_target_pairs={{0,16},{4,20},{8,24},{12,28},{16,0},{20,4},{24,8},{28,12},{32,48},... | collective-permute-start | bytes 9437192 | tf_op jit(solution)/shard_map/ppermute | solution.py:23
  699.3 68.5 %collective-permute-start.3 = (f32[768,1024]{0,1:T(8,128)S(1)}, f32[768,1024]{0,1:T(8,128)S(1)}, u32[]{:S(2)}, u32[]{:S(2)}) collective-permute-start(f32[768,1024]{0,1:T(8,128)S(1)} %add.41), channel_id=1, source_target_pairs={{0,32},{4,36},{8,40},{12,44},{16,48},{20,52},{24,56},{28,60},{32,0... | collective-permute-start | bytes 9437192 | tf_op jit(solution)/shard_map/ppermute | solution.py:23
  769.9 69.4 %collective-permute-start.4 = (f32[768,1024]{0,1:T(8,128)}, f32[768,1024]{0,1:T(8,128)}, u32[]{:S(2)}, u32[]{:S(2)}) collective-permute-start(f32[768,1024]{0,1:T(8,128)} %add.42), channel_id=1, source_target_pairs={{0,64},{4,68},{8,72},{12,76},{16,80},{20,84},{24,88},{28,92},{32,9... | collective-permute-start | bytes 9437192 | tf_op jit(solution)/shard_map/ppermute | solution.py:23
Sparse Core Ops, SparseCore 0:
  19.7 82.2 all-gather.6
  109.1 123.3 all-gather.8
  237.0 128.3 all-gather.10
  390.3 158.9 reduce-scatter.1
